TPU v7x, 32 devices: a whole 2x2x4 slice. The times are simulated.
32 devices in a mesh: date: 2 (over y), slab: 16 (over z, x, core).
Axes of the slice: x: 2, y: 2, z: 4, core: 2. Of those that a mesh axis runs over, the one named last changes fastest.
Arguments:
- pressure: float32 [16, 12288], P('slab', 'date'), parts along dimension 1, may hold values from -6 to 6
- density: float32 [16, 12288], P('slab', 'date'), parts along dimension 1, may hold values from -6 to 6
- vertical_wind: float32 [16, 12288], P('slab', 'date'), parts along dimension 1, may hold values from -6 to 6
- horizontal_wind: float32 [2, 16, 12288], P(None, 'slab', 'date'), parts along dimension 2, may hold values from -6 to 6
- metric_terms: float32 [2, 6144], replicated, may hold values from 0.25 to 1
- neighbors: int32 [4, 6144], replicated, may hold values from 0 to 6143, as said below
- level_order: int32 [16], replicated, may hold values from 0 to 15, each once
- stiffness: float32 [16], replicated, may hold values from 0.2 to 5
- coupling: float32 [16], replicated, may hold values from 0.2 to 1
- weight_one: bfloat16 [64, 512], P('slab'), may hold values from -0.75 to 0.75
- weight_two: bfloat16 [512, 512], P('slab'), may hold values from -0.25 to 0.25
- weight_three: bfloat16 [512, 16], P('slab'), may hold values from -0.25 to 0.25
- pressure_adjoint: float32 [16, 12288], P('slab', 'date'), parts along dimension 1, may hold values from -6 to 6
- wind_adjoint: float32 [16, 12288], P('slab', 'date'), parts along dimension 1, may hold values from -6 to 6
Outputs:
- pressure_new: float32 [16, 12288], P('slab', 'date'), parts along dimension 1
- wind_new: float32 [16, 12288], P('slab', 'date'), parts along dimension 1
- pressure_grad: float32 [16, 12288], P('slab', 'date'), parts along dimension 1
- first_grad: float32 [128, 512], P(('date', 'slab')), parts along dimension 0
- second_grad: float32 [1024, 512], P(('date', 'slab')), parts along dimension 0
- third_grad: float32 [1024, 16], P(('date', 'slab')), parts along dimension 0
There are 2 independent parts, one for each index of `date`. A program takes and returns all parts, laid end to end along the dimension named above; an argument that names none is the same for every part. Nothing has to cross between parts.
Inputs may be any that keep to these rules, and one draw needn't show every extreme that they name: `neighbors`: the columns are the cells of a 8 x 768 grid stored in some order; rows 0, 1, 2, 3 give the stored positions of a column's east, west, north and south neighbours, and the column itself where the grid's edge lies on that side. `level_order`: each level appears once.
All inputs are finite; a program needn't handle non-finite values.
Results may differ from a plain program's by a relative error of at most 0.0075.
Values may be sent and summed in bfloat16 or wider, within the bound.
No kernel may reach another device: no remote copies, remote signals or barrier semaphores. Data moves between devices by JAX's collectives and lax.ppermute only.
A program may use at most 128 MiB of HBM per device.

v0:
```python
import math
import jax
import jax.numpy as jnp
from jax import lax
from jax.sharding import PartitionSpec as P


def lower_diff(field):
    return jnp.concatenate([field[1:] - field[:-1], -field[-1:]], axis=0)


def upper_diff(field):
    return jnp.concatenate([jnp.zeros_like(field[:1]), field[:-1]], axis=0) - field


def level_inverse(stiffness):
    below = jnp.concatenate([jnp.zeros((1,), jnp.float32), stiffness[:-1]])
    matrix = (
        jnp.diag(1.0 + stiffness + below)
        - jnp.diag(stiffness[:-1], 1)
        - jnp.diag(stiffness[:-1], -1)
    )
    factor = jnp.linalg.cholesky(matrix)
    identity = jnp.eye(stiffness.shape[0], dtype=jnp.float32)
    return jax.scipy.linalg.cho_solve((factor, True), identity)


def apply_inverse(inverse_matrix, rhs):
    return jnp.dot(
        inverse_matrix, rhs, precision=lax.Precision.HIGHEST, preferred_element_type=jnp.float32
    )


def contract_first(left, right):
    return lax.dot_general(
        left, right, (((0,), (0,)), ((), ())), preferred_element_type=jnp.float32
    )


def contract_last(left, right):
    return lax.dot_general(
        left, right, (((1,), (1,)), ((), ())), preferred_element_type=jnp.float32
    )


def body(
    pressure,
    density,
    vertical_wind,
    horizontal_wind,
    metric_terms,
    neighbors,
    level_order,
    stiffness,
    coupling,
    weight_one,
    weight_two,
    weight_three,
    pressure_adjoint,
    wind_adjoint,
):
    east = jnp.take(horizontal_wind[0], neighbors[0], axis=1)
    west = jnp.take(horizontal_wind[0], neighbors[1], axis=1)
    north = jnp.take(horizontal_wind[1], neighbors[2], axis=1)
    south = jnp.take(horizontal_wind[1], neighbors[3], axis=1)
    diverg = metric_terms[0] * (east - west) + metric_terms[1] * (north - south)
    star = pressure - diverg
    inverse = jnp.argsort(level_order)
    scale = 1.0 / math.sqrt(neighbors.shape[1])
    forward_raw = lax.all_to_all(
        jnp.stack([star, density, vertical_wind, diverg]).astype(jnp.bfloat16),
        "slab",
        split_axis=2,
        concat_axis=1,
        tiled=True,
    ).astype(jnp.float32)
    full_one, full_two, full_three = (
        lax.all_gather(weight_one, "slab", axis=0, tiled=True),
        lax.all_gather(weight_two, "slab", axis=0, tiled=True),
        lax.all_gather(weight_three, "slab", axis=0, tiled=True),
    )
    forward_part = jnp.take(forward_raw, inverse, axis=1)
    levels = forward_part.shape[1]
    width = forward_part.shape[2]
    couple = coupling[:, None]
    column_input = forward_part.reshape(4 * levels, width).astype(jnp.bfloat16)
    pre_one = contract_first(full_one, column_input)
    tanh_one = jnp.tanh(pre_one)
    act_one = tanh_one.astype(jnp.bfloat16)
    pre_two = contract_first(full_two, act_one)
    tanh_two = jnp.tanh(pre_two)
    act_two = tanh_two.astype(jnp.bfloat16)
    heating = contract_first(full_three, act_two)
    star_column = forward_part[0]
    rhs = forward_part[2] - couple * lower_diff(star_column) - 0.5 * forward_part[1] + heating
    inverse_matrix = level_inverse(stiffness)
    wind_next = apply_inverse(inverse_matrix, rhs)
    press_next = star_column + upper_diff(couple * wind_next)
    forward_slabs = lax.all_to_all(
        jnp.take(jnp.stack([press_next, wind_next]), level_order, axis=1).astype(jnp.bfloat16),
        "slab",
        split_axis=1,
        concat_axis=2,
        tiled=True,
    ).astype(jnp.float32)
    adjoint_raw = lax.all_to_all(
        jnp.stack([pressure_adjoint, wind_adjoint]), "slab", split_axis=2, concat_axis=1, tiled=True
    )
    adjoint_part = jnp.take(adjoint_raw, inverse, axis=1)
    wind_grad = adjoint_part[1] + couple * lower_diff(adjoint_part[0])
    rhs_grad = apply_inverse(inverse_matrix, wind_grad)
    star_grad = adjoint_part[0] - upper_diff(couple * rhs_grad)
    heat_grad = rhs_grad.astype(jnp.bfloat16)
    local_three = contract_last(act_two, heat_grad) * scale
    back_two = jnp.dot(full_three, heat_grad, preferred_element_type=jnp.float32)
    pre_two_grad = (back_two * (1.0 - tanh_two * tanh_two)).astype(jnp.bfloat16)
    local_two = contract_last(act_one, pre_two_grad) * scale
    back_one = jnp.dot(full_two, pre_two_grad, preferred_element_type=jnp.float32)
    pre_one_grad = (back_one * (1.0 - tanh_one * tanh_one)).astype(jnp.bfloat16)
    local_one = contract_last(column_input, pre_one_grad) * scale
    first_grad, second_grad, third_grad = (
        lax.psum_scatter(local_one, "slab", scatter_dimension=0, tiled=True),
        lax.psum_scatter(local_two, "slab", scatter_dimension=0, tiled=True),
        lax.psum_scatter(local_three, "slab", scatter_dimension=0, tiled=True),
    )
    input_grad = jnp.dot(full_one, pre_one_grad, preferred_element_type=jnp.float32)
    star_grad = star_grad + input_grad[:levels]
    stored_grad = jnp.take(star_grad, level_order, axis=0)
    pressure_new = forward_slabs[0]
    wind_new = forward_slabs[1]
    pressure_grad = lax.all_to_all(
        stored_grad[None].astype(jnp.bfloat16), "slab", split_axis=1, concat_axis=2, tiled=True
    ).astype(jnp.float32)[0]
    return (pressure_new, wind_new, pressure_grad, first_grad, second_grad, third_grad)


def solution(mesh):
    in_specs = (
        P("slab", "date"),
        P("slab", "date"),
        P("slab", "date"),
        P(None, "slab", "date"),
        P(),
        P(),
        P(),
        P(),
        P(),
        P("slab", None),
        P("slab", None),
        P("slab", None),
        P("slab", "date"),
        P("slab", "date"),
    )
    out_specs = (
        P("slab", "date"),
        P("slab", "date"),
        P("slab", "date"),
        P(("date", "slab"), None),
        P(("date", "slab"), None),
        P(("date", "slab"), None),
    )
    return jax.shard_map(body, mesh=mesh, in_specs=in_specs, out_specs=out_specs, check_vma=False)
```

profile of v0, /device:TPU:0, one launch (start us, length us, event | category | flops | bytes accessed | tf_op | source)
XLA Modules:
  0.0 540.4 jit_solution(8033137742579381662)
XLA Ops:
  9.1 34.3 %gather_fusion.4 = f32[6144]{0:T(1024)S(1)} fusion(f32[6144]{0:T(1024)S(1)} %bitcast.140, s32[6144]{0:T(1024)S(1)} %fusion.25), kind=kCustom, calls=%fused_computation.3.clone | custom fusion | bytes 73728 | tf_op jit(solution)/shard_map/jit(_take)/gather | solution.py:64
  43.5 34.3 %gather_fusion.5 = f32[6144]{0:T(1024)S(1)} fusion(f32[6144]{0:T(1024)S(1)} %bitcast.141, s32[6144]{0:T(1024)S(1)} %fusion.26), kind=kCustom, calls=%fused_computation.4.clone | custom fusion | bytes 73728 | tf_op jit(solution)/shard_map/jit(_take)/gather | solution.py:65
  77.8 34.3 %gather_fusion.2 = f32[6144]{0:T(1024)S(1)} fusion(f32[6144]{0:T(1024)S(1)} %bitcast.138, s32[6144]{0:T(1024)S(1)} %fusion.23), kind=kCustom, calls=%fused_computation.clone | custom fusion | bytes 73728 | tf_op jit(solution)/shard_map/jit(_take)/gather | solution.py:62
  112.2 34.3 %gather_fusion.3 = f32[6144]{0:T(1024)S(1)} fusion(f32[6144]{0:T(1024)S(1)} %bitcast.139, s32[6144]{0:T(1024)S(1)} %fusion.24), kind=kCustom, calls=%fused_computation.2.clone | custom fusion | bytes 73728 | tf_op jit(solution)/shard_map/jit(_take)/gather | solution.py:63
  146.9 4.0 copy.50
  151.5 34.5 %reduce.6 = bf16[6144,4]{1,0:T(8,128)(2,1)} reduce(bf16[6144,1,4]{2,1,0:T(2,128)(2,1)S(1)} %bitcast.142, bf16[]{:T(256)} %broadcast.246), dimensions={1}, to_apply=%bitcast.107.reduce_sub_computation | reduce | bytes 98306
  186.0 4.4 reshape.350
  190.4 7.4 %all-to-all-start = ((bf16[16,2,768]{2,1,0:T(2,128)(2,1)}), bf16[16,2,768]{2,1,0:T(2,128)(2,1)S(1)}, u32[]{:S(2)}, u32[]{:S(2)}) async-start(bf16[16,2,768]{2,1,0:T(2,128)(2,1)} %reshape.350), calls=%async_computation | async-start | bytes 98304 | tf_op jit(solution)/shard_map/all_to_all | solution.py:70
  199.2 21.9 %all-gather = bf16[16,4,512]{2,1,0:T(4,128)(2,1)S(1)} all-gather(bf16[1,4,512]{2,1,0:T(4,128)(2,1)S(1)} %bitcast.168), channel_id=1, replica_groups=mesh['date'=2,'slab'=16] {'slab'}, dimensions={0}, use_global_device_ids=true | all-gather | bytes 69632 | tf_op jit(solution)/shard_map/all_gather | solution.py:78
  221.1 20.3 %all_gather.10 = bf16[512,512]{1,0:T(8,128)(2,1)} all-gather(bf16[32,512]{1,0:T(8,128)(2,1)S(1)} %copy-done.2), channel_id=1, replica_groups=mesh['date'=2,'slab'=16] {'slab'}, dimensions={0}, use_global_device_ids=true | all-gather | bytes 557056 | tf_op jit(solution)/shard_map/all_gather | solution.py:79
  241.4 19.3 %all-gather.1 = bf16[16,32,16]{1,2,0:T(8,128)(2,1)S(1)} all-gather(bf16[1,32,16]{1,2,0:T(8,128)(2,1)S(1)} %bitcast.169), channel_id=1, replica_groups=mesh['date'=2,'slab'=16] {'slab'}, dimensions={0}, use_global_device_ids=true | all-gather | bytes 17408 | tf_op jit(solution)/shard_map/all_gather | solution.py:80
  265.4 3.3 copy.56
  269.2 28.4 %reduce.7 = f32[6144,2]{1,0:T(8,128)} reduce(f32[6144,1,2]{2,1,0:T(1,128)S(1)} %bitcast.143, f32[]{:T(128)} %broadcast.247), dimensions={1}, to_apply=%bitcast.109.reduce_sub_computation | reduce | bytes 98308
  297.6 4.3 reshape.352
  302.0 3.5 all-to-all-start.2
  305.7 4.0 reshape.351
  314.2 4.5 reshape.353
  329.7 6.0 %all-to-all-start.3 = ((bf16[16,2,192]{2,1,0:T(2,128)(2,1)}), bf16[16,2,192]{2,1,0:T(2,128)(2,1)S(1)}, u32[]{:S(2)}, u32[]{:S(2)}) async-start(bf16[16,2,192]{2,1,0:T(2,128)(2,1)} %reshape.354), calls=%async_computation.3 | async-start | bytes 32768 | tf_op jit(solution)/shard_map/all_to_all | solution.py:131
  337.0 5.1 all-to-all-done.3
  342.2 3.5 all-to-all-start.1
  347.7 4.5 all-to-all-done.1
  352.8 28.3 %reduce-scatter.7.cloned.1.call-done = f32[32,16]{1,0:T(8,128)} async-done(((f32[512,16]{1,0:T(8,128)}), f32[32,16]{1,0:T(8,128)}) %reduce-scatter.7.cloned.1.call-update) | async-done | bytes 2064
  382.5 88.1 %all-reduce.6.cloned.1.call-done = f32[64,512]{1,0:T(8,128)} async-done(((f32[64,512]{1,0:T(8,128)}), f32[64,512]{1,0:T(8,128)}) %all-reduce.6.cloned.1.call-update) | async-done | bytes 131088
  472.0 61.9 %reduce-scatter.5.cloned.1.call-done = f32[32,512]{1,0:T(8,128)} async-done(((f32[512,512]{1,0:T(8,128)}), f32[32,512]{1,0:T(8,128)}) %reduce-scatter.5.cloned.1.call-update) | async-done | bytes 65552 | tf_op jit(solution)/shard_map/reduce_scatter | solution.py:123
  (121 shorter events, 31.1 us)
Async XLA Ops:
  112.1 34.4 %copy-start.4 = (f32[1,6144]{1,0:T(1,128)S(1)}, f32[1,6144]{1,0:T(1,128)}, u32[]{:S(2)}) copy-start(f32[1,6144]{1,0:T(1,128)} %param.19) | copy-start | bytes 73732
  112.1 34.4 %copy-start.1 = (f32[2,6144]{1,0:T(2,128)S(1)}, f32[2,6144]{1,0:T(2,128)}, u32[]{:S(2)}) copy-start(f32[2,6144]{1,0:T(2,128)} %param.22) | copy-start | bytes 147460
  112.1 34.4 %copy-start.3 = (f32[1,6144]{1,0:T(1,128)S(1)}, f32[1,6144]{1,0:T(1,128)}, u32[]{:S(2)}) copy-start(f32[1,6144]{1,0:T(1,128)} %param.18) | copy-start | bytes 73732
  112.1 34.5 %copy-start.5 = (f32[1,6144]{1,0:T(1,128)S(1)}, f32[1,6144]{1,0:T(1,128)}, u32[]{:S(2)}) copy-start(f32[1,6144]{1,0:T(1,128)} %param.20) | copy-start | bytes 73732
  151.4 46.3 %copy-start.13 = (s32[16]{0:T(128)S(1)}, s32[16]{0:T(128)}, u32[]{:S(2)}) copy-start(s32[16]{0:T(128)} %param.24) | copy-start | bytes 196
  151.5 47.7 %copy-start.8 = (bf16[4,512]{1,0:T(4,128)(2,1)S(1)}, bf16[4,512]{1,0:T(4,128)(2,1)}, u32[]{:S(2)}) copy-start(bf16[4,512]{1,0:T(4,128)(2,1)} %param.27) | copy-start | bytes 12292
  151.5 69.6 %copy-start.2 = (bf16[32,512]{1,0:T(8,128)(2,1)S(1)}, bf16[32,512]{1,0:T(8,128)(2,1)}, u32[]{:S(2)}) copy-start(bf16[32,512]{1,0:T(8,128)(2,1)} %param.28) | copy-start | bytes 98308
  151.5 89.9 %copy-start.9 = (bf16[32,16]{0,1:T(8,128)(2,1)S(1)}, bf16[32,16]{0,1:T(8,128)(2,1)}, u32[]{:S(2)}) copy-start(bf16[32,16]{0,1:T(8,128)(2,1)} %param.29) | copy-start | bytes 3076
  151.5 109.3 %copy-start.10 = (f32[16]{0:T(128)S(1)}, f32[16]{0:T(128)}, u32[]{:S(2)}) copy-start(f32[16]{0:T(128)} %param.25) | copy-start | bytes 196
  151.5 109.3 %copy-start.12 = (pred[16]{0:T(512)(128)(4,1)S(1)}, pred[16]{0:T(512)(128)(4,1)}, u32[]{:S(2)}) copy-start(pred[16]{0:T(512)(128)(4,1)} %constant.116.clone.1) | copy-start | bytes 52
  151.5 113.9 %copy-start.6 = (f32[1,6144]{1,0:T(1,128)S(1)}, f32[1,6144]{1,0:T(1,128)}, u32[]{:S(2)}) copy-start(f32[1,6144]{1,0:T(1,128)} %param.31) | copy-start | bytes 73732
  151.5 113.9 %copy-start.7 = (f32[1,6144]{1,0:T(1,128)S(1)}, f32[1,6144]{1,0:T(1,128)}, u32[]{:S(2)}) copy-start(f32[1,6144]{1,0:T(1,128)} %param.30) | copy-start | bytes 73732
  190.4 111.6 %all-to-all-start = ((bf16[16,2,768]{2,1,0:T(2,128)(2,1)}), bf16[16,2,768]{2,1,0:T(2,128)(2,1)S(1)}, u32[]{:S(2)}, u32[]{:S(2)}) async-start(bf16[16,2,768]{2,1,0:T(2,128)(2,1)} %reshape.350), calls=%async_computation | async-start | bytes 98304 | tf_op jit(solution)/shard_map/all_to_all | solution.py:70
  302.0 11.4 %all-to-all-start.2 = ((f32[16,1,768]{2,1,0:T(1,128)}), f32[16,1,768]{2,1,0:T(1,128)S(1)}, u32[]{:S(2)}, u32[]{:S(2)}) async-start(f32[16,1,768]{2,1,0:T(1,128)} %reshape.352), calls=%async_computation.2 | async-start | bytes 98304 | tf_op jit(solution)/shard_map/all_to_all | solution.py:106
  305.5 75.7 %reduce-scatter.7.cloned.1.call-start = ((), (), s32[]{:S(2)}) async-start(), calls=%async_computation.7 | async-start | bytes 278528
  318.7 3.7 copy-start.11
  320.7 3.8 copy-start
  324.4 146.2 %all-reduce.6.cloned.1.call-start = ((), (), s32[]{:S(2)}) async-start(), calls=%async_computation.8 | async-start | bytes 262144
  324.9 20.8 %copy-start.14 = (u32[32]{0:T(128)S(1)}, u32[32]{0:T(128)}, u32[]{:S(2)}) copy-start(u32[32]{0:T(128)} %constant.136) | copy-start | bytes 388
  325.8 208.2 %reduce-scatter.5.cloned.1.call-start = ((), (), s32[]{:S(2)}) async-start(), calls=%async_computation.6 | async-start | bytes 1114112 | tf_op jit(solution)/shard_map/reduce_scatter | solution.py:123
  329.7 12.5 %all-to-all-start.3 = ((bf16[16,2,192]{2,1,0:T(2,128)(2,1)}), bf16[16,2,192]{2,1,0:T(2,128)(2,1)S(1)}, u32[]{:S(2)}, u32[]{:S(2)}) async-start(bf16[16,2,192]{2,1,0:T(2,128)(2,1)} %reshape.354), calls=%async_computation.3 | async-start | bytes 32768 | tf_op jit(solution)/shard_map/all_to_all | solution.py:131
  342.2 10.0 %all-to-all-start.1 = ((bf16[2,16,384]{2,0,1:T(2,128)(2,1)}), bf16[2,16,384]{2,0,1:T(2,128)(2,1)S(1)}, u32[]{:S(2)}, u32[]{:S(2)}) async-start(bf16[2,16,384]{2,0,1:T(2,128)(2,1)} %bitcast_convert_fusion), calls=%async_computation.1 | async-start | bytes 49152 | tf_op jit(solution)/shard_map/all_to_all | solution.py:99
Sparse Core Ops, SparseCore 0:
  324.5 56.5 reduce-scatter.6
  384.6 86.0 all-reduce.5
  474.8 59.0 reduce-scatter.4
where the time goes:
time: 541 us; the launch traced here: 540 us
  waiting for transfers between devices  188 us (35%)
  local copies, waits for them, and re-layouts  177 us (33%)
  other arithmetic  72 us (13%)
  blocking collectives  61.4 us (11%)
  starting transfers between devices  20.7 us (4%)
  between operations  15 us (3%)
  matrix products  6.09 us (1%)
    unnamed x5, waiting for transfers between devices  116 us
    unnamed x3, other arithmetic  63.6 us
    reduce_scatter x1, waiting for transfers between devices, body(): lax.psum_scatter(local_two, 'slab', scatter_dimension=0, tiled=True)  61.9 us
    gather x1, local copies, waits for them, and re-layouts, body(): south = jnp.take(horizontal_wind[1], neighbors[3], axis=1)  34.3 us
    gather x1, local copies, waits for them, and re-layouts, body(): east = jnp.take(horizontal_wind[0], neighbors[0], axis=1)  34.3 us
    gather x1, local copies, waits for them, and re-layouts, body(): west = jnp.take(horizontal_wind[0], neighbors[1], axis=1)  34.3 us
    gather x1, local copies, waits for them, and re-layouts, body(): north = jnp.take(horizontal_wind[1], neighbors[2], axis=1)  34.3 us
    unnamed x44, local copies, waits for them, and re-layouts  23.4 us
  transfers between devices with their start and end apart: 7, of which 5 were waited for; matrix products, arithmetic and copies ran while one was open for 11% of the time, Pallas kernels for 0%

commit v1 on v0

--- a/solution.py
+++ b/solution.py
@@ -3,6 +3,13 @@
 import jax.numpy as jnp
 from jax import lax
 from jax.sharding import PartitionSpec as P
+
+fit_lanes = lambda my_tile, axis_key: jnp.concatenate(
+    jax.lax.all_to_all(
+        jnp.stack(jnp.split(my_tile, jax.lax.axis_size(axis_key), 1), axis=0), axis_key, 0, 0
+    ),
+    2,
+)
 
 
 def lower_diff(field):
@@ -128,9 +135,7 @@
     stored_grad = jnp.take(star_grad, level_order, axis=0)
     pressure_new = forward_slabs[0]
     wind_new = forward_slabs[1]
-    pressure_grad = lax.all_to_all(
-        stored_grad[None].astype(jnp.bfloat16), "slab", split_axis=1, concat_axis=2, tiled=True
-    ).astype(jnp.float32)[0]
+    pressure_grad = fit_lanes(stored_grad[None].astype(jnp.bfloat16), "slab").astype(jnp.float32)[0]
     return (pressure_new, wind_new, pressure_grad, first_grad, second_grad, third_grad)
 
 

time: 541 us -> 547 us (1.011)
    unnamed x3 -> x2, other arithmetic: 63.6 us -> 62.8 us
    unnamed x44 -> x71, local copies, waits for them, and re-layouts: 23.4 us -> 23.6 us
where the time goes in v1:
time: 547 us; the launch traced here: 546 us
  waiting for transfers between devices  191 us (35%)
  local copies, waits for them, and re-layouts  178 us (33%)
  other arithmetic  73.4 us (13%)
  blocking collectives  61.4 us (11%)
  starting transfers between devices  20.7 us (4%)
  between operations  15 us (3%)
  matrix products  6.11 us (1%)
    unnamed x5, waiting for transfers between devices  119 us
    unnamed x2, other arithmetic  62.8 us
    reduce_scatter x1, waiting for transfers between devices, body(): lax.psum_scatter(local_two, 'slab', scatter_dimension=0, tiled=True)  61.9 us
    gather x1, local copies, waits for them, and re-layouts, body(): east = jnp.take(horizontal_wind[0], neighbors[0], axis=1)  34.3 us
    gather x1, local copies, waits for them, and re-layouts, body(): west = jnp.take(horizontal_wind[0], neighbors[1], axis=1)  34.3 us
    gather x1, local copies, waits for them, and re-layouts, body(): north = jnp.take(horizontal_wind[1], neighbors[2], axis=1)  34.3 us
    gather x1, local copies, waits for them, and re-layouts, body(): south = jnp.take(horizontal_wind[1], neighbors[3], axis=1)  34.3 us
    unnamed x71, local copies, waits for them, and re-layouts  23.6 us
  transfers between devices with their start and end apart: 7, of which 5 were waited for; matrix products, arithmetic and copies ran while one was open for 11% of the time, Pallas kernels for 0%

profile of v1, /device:TPU:0, one launch (start us, length us, event | category | flops | bytes accessed | tf_op | source)
XLA Modules:
  0.0 545.8 jit_solution(1739755569360778780)
XLA Ops:
  9.1 34.3 %gather_fusion.4 = f32[6144]{0:T(1024)S(1)} fusion(f32[6144]{0:T(1024)S(1)} %bitcast.201, s32[6144]{0:T(1024)S(1)} %get-tuple-element.30), kind=kCustom, calls=%fused_computation.3.clone | custom fusion | bytes 73728 | tf_op jit(solution)/shard_map/jit(_take)/gather | solution.py:71
  43.4 34.3 %gather_fusion.5 = f32[6144]{0:T(1024)S(1)} fusion(f32[6144]{0:T(1024)S(1)} %bitcast.202, s32[6144]{0:T(1024)S(1)} %get-tuple-element.31), kind=kCustom, calls=%fused_computation.4.clone | custom fusion | bytes 73728 | tf_op jit(solution)/shard_map/jit(_take)/gather | solution.py:72
  77.8 34.3 %gather_fusion.2 = f32[6144]{0:T(1024)S(1)} fusion(f32[6144]{0:T(1024)S(1)} %bitcast.199, s32[6144]{0:T(1024)S(1)} %get-tuple-element.28), kind=kCustom, calls=%fused_computation.clone | custom fusion | bytes 73728 | tf_op jit(solution)/shard_map/jit(_take)/gather | solution.py:69
  112.1 34.3 %gather_fusion.3 = f32[6144]{0:T(1024)S(1)} fusion(f32[6144]{0:T(1024)S(1)} %bitcast.200, s32[6144]{0:T(1024)S(1)} %get-tuple-element.29), kind=kCustom, calls=%fused_computation.2.clone | custom fusion | bytes 73728 | tf_op jit(solution)/shard_map/jit(_take)/gather | solution.py:70
  146.8 4.0 copy.48
  151.4 34.5 %reduce.6 = bf16[6144,4]{1,0:T(8,128)(2,1)} reduce(bf16[6144,1,4]{2,1,0:T(2,128)(2,1)S(1)} %bitcast.203, bf16[]{:T(256)} %broadcast.246), dimensions={1}, to_apply=%bitcast.171.reduce_sub_computation | reduce | bytes 98306
  186.0 4.4 reshape.348
  190.3 7.4 %all-to-all-start = ((bf16[16,2,768]{2,1,0:T(2,128)(2,1)}), bf16[16,2,768]{2,1,0:T(2,128)(2,1)S(1)}, u32[]{:S(2)}, u32[]{:S(2)}) async-start(bf16[16,2,768]{2,1,0:T(2,128)(2,1)} %reshape.348), calls=%async_computation | async-start | bytes 98304 | tf_op jit(solution)/shard_map/all_to_all | solution.py:77
  200.2 21.9 %all-gather = bf16[16,4,512]{2,1,0:T(4,128)(2,1)S(1)} all-gather(bf16[1,4,512]{2,1,0:T(4,128)(2,1)S(1)} %bitcast.229), channel_id=1, replica_groups=mesh['date'=2,'slab'=16] {'slab'}, dimensions={0}, use_global_device_ids=true | all-gather | bytes 69632 | tf_op jit(solution)/shard_map/all_gather | solution.py:85
  222.1 20.3 %all_gather.10 = bf16[512,512]{1,0:T(8,128)(2,1)} all-gather(bf16[32,512]{1,0:T(8,128)(2,1)S(1)} %copy-done.2), channel_id=1, replica_groups=mesh['date'=2,'slab'=16] {'slab'}, dimensions={0}, use_global_device_ids=true | all-gather | bytes 557056 | tf_op jit(solution)/shard_map/all_gather | solution.py:86
  242.3 19.3 %all-gather.1 = bf16[16,32,16]{1,2,0:T(8,128)(2,1)S(1)} all-gather(bf16[1,32,16]{1,2,0:T(8,128)(2,1)S(1)} %bitcast.230), channel_id=1, replica_groups=mesh['date'=2,'slab'=16] {'slab'}, dimensions={0}, use_global_device_ids=true | all-gather | bytes 17408 | tf_op jit(solution)/shard_map/all_gather | solution.py:87
  266.4 3.3 copy.54
  270.2 28.3 %reduce.7 = f32[6144,2]{1,0:T(8,128)} reduce(f32[6144,1,2]{2,1,0:T(1,128)S(1)} %bitcast.204, f32[]{:T(128)} %broadcast.247), dimensions={1}, to_apply=%bitcast.173.reduce_sub_computation | reduce | bytes 98308
  298.5 4.3 reshape.350
  303.4 3.5 all-to-all-start.2
  307.2 4.0 reshape.349
  316.1 4.5 reshape.351
  332.9 6.0 %all-to-all-start.3 = ((bf16[16,2,192]{2,1,0:T(2,128)(2,1)}), bf16[16,2,192]{2,1,0:T(2,128)(2,1)S(1)}, u32[]{:S(2)}, u32[]{:S(2)}) async-start(bf16[16,2,192]{2,1,0:T(2,128)(2,1)} %reshape.352), calls=%async_computation.3 | async-start | bytes 32768 | tf_op jit(solution)/shard_map/all_to_all | solution.py:8
  340.4 5.0 all-to-all-done.3
  345.4 3.5 all-to-all-start.1
  350.9 4.5 all-to-all-done.1
  356.1 30.3 %reduce-scatter.7.cloned.1.call-done = f32[32,16]{1,0:T(8,128)} async-done(((f32[512,16]{1,0:T(8,128)}), f32[32,16]{1,0:T(8,128)}) %reduce-scatter.7.cloned.1.call-update) | async-done | bytes 2064
  387.8 88.1 %all-reduce.6.cloned.1.call-done = f32[64,512]{1,0:T(8,128)} async-done(((f32[64,512]{1,0:T(8,128)}), f32[64,512]{1,0:T(8,128)}) %all-reduce.6.cloned.1.call-update) | async-done | bytes 131088
  477.3 61.9 %reduce-scatter.5.cloned.1.call-done = f32[32,512]{1,0:T(8,128)} async-done(((f32[512,512]{1,0:T(8,128)}), f32[32,512]{1,0:T(8,128)}) %reduce-scatter.5.cloned.1.call-update) | async-done | bytes 65552 | tf_op jit(solution)/shard_map/reduce_scatter | solution.py:130
  (144 shorter events, 34.5 us)
Async XLA Ops:
  112.1 34.4 %copy-start.4 = (f32[1,6144]{1,0:T(1,128)S(1)}, f32[1,6144]{1,0:T(1,128)}, u32[]{:S(2)}) copy-start(f32[1,6144]{1,0:T(1,128)} %param.20) | copy-start | bytes 73732
  112.1 34.4 %copy-start.5 = (f32[1,6144]{1,0:T(1,128)S(1)}, f32[1,6144]{1,0:T(1,128)}, u32[]{:S(2)}) copy-start(f32[1,6144]{1,0:T(1,128)} %param.19) | copy-start | bytes 73732
  112.1 34.4 %copy-start.1 = (f32[2,6144]{1,0:T(2,128)S(1)}, f32[2,6144]{1,0:T(2,128)}, u32[]{:S(2)}) copy-start(f32[2,6144]{1,0:T(2,128)} %param.22) | copy-start | bytes 147460
  112.1 34.4 %copy-start.3 = (f32[1,6144]{1,0:T(1,128)S(1)}, f32[1,6144]{1,0:T(1,128)}, u32[]{:S(2)}) copy-start(f32[1,6144]{1,0:T(1,128)} %param.18) | copy-start | bytes 73732
  151.4 46.3 %copy-start.19 = (s32[16]{0:T(128)S(1)}, s32[16]{0:T(128)}, u32[]{:S(2)}) copy-start(s32[16]{0:T(128)} %param.24) | copy-start | bytes 196
  151.4 48.8 %copy-start.10 = (bf16[4,512]{1,0:T(4,128)(2,1)S(1)}, bf16[4,512]{1,0:T(4,128)(2,1)}, u32[]{:S(2)}) copy-start(bf16[4,512]{1,0:T(4,128)(2,1)} %param.27) | copy-start | bytes 12292
  151.4 70.7 %copy-start.2 = (bf16[32,512]{1,0:T(8,128)(2,1)S(1)}, bf16[32,512]{1,0:T(8,128)(2,1)}, u32[]{:S(2)}) copy-start(bf16[32,512]{1,0:T(8,128)(2,1)} %param.28) | copy-start | bytes 98308
  151.4 90.9 %copy-start.11 = (bf16[32,16]{0,1:T(8,128)(2,1)S(1)}, bf16[32,16]{0,1:T(8,128)(2,1)}, u32[]{:S(2)}) copy-start(bf16[32,16]{0,1:T(8,128)(2,1)} %param.29) | copy-start | bytes 3076
  151.4 110.4 %copy-start.15 = (f32[16]{0:T(128)S(1)}, f32[16]{0:T(128)}, u32[]{:S(2)}) copy-start(f32[16]{0:T(128)} %param.25) | copy-start | bytes 196
  151.4 110.4 %copy-start.18 = (pred[16]{0:T(512)(128)(4,1)S(1)}, pred[16]{0:T(512)(128)(4,1)}, u32[]{:S(2)}) copy-start(pred[16]{0:T(512)(128)(4,1)} %constant.116.clone.1) | copy-start | bytes 52
  151.4 114.9 %copy-start.6 = (f32[1,6144]{1,0:T(1,128)S(1)}, f32[1,6144]{1,0:T(1,128)}, u32[]{:S(2)}) copy-start(f32[1,6144]{1,0:T(1,128)} %param.31) | copy-start | bytes 73732
  151.4 114.9 %copy-start.7 = (f32[1,6144]{1,0:T(1,128)S(1)}, f32[1,6144]{1,0:T(1,128)}, u32[]{:S(2)}) copy-start(f32[1,6144]{1,0:T(1,128)} %param.30) | copy-start | bytes 73732
  190.3 113.1 %all-to-all-start = ((bf16[16,2,768]{2,1,0:T(2,128)(2,1)}), bf16[16,2,768]{2,1,0:T(2,128)(2,1)S(1)}, u32[]{:S(2)}, u32[]{:S(2)}) async-start(bf16[16,2,768]{2,1,0:T(2,128)(2,1)} %reshape.348), calls=%async_computation | async-start | bytes 98304 | tf_op jit(solution)/shard_map/all_to_all | solution.py:77
  199.0 115.7 %copy-start.12 = (pred[16]{0:T(512)(128)(4,1)}, pred[16]{0:T(512)(128)(4,1)S(1)}, u32[]{:S(2)}) copy-start(pred[16]{0:T(512)(128)(4,1)S(1)} %compare_and_fusion.1) | copy-start | bytes 52
  303.4 10.7 %copy-start.8 = (s32[1024]{0:T(1024)}, s32[1024]{0:T(1024)S(1)}, u32[]{:S(2)}) copy-start(s32[1024]{0:T(1024)S(1)} %get-tuple-element.33) | copy-start | bytes 12292
  303.4 12.0 %all-to-all-start.2 = ((f32[16,1,768]{2,1,0:T(1,128)}), f32[16,1,768]{2,1,0:T(1,128)S(1)}, u32[]{:S(2)}, u32[]{:S(2)}) async-start(f32[16,1,768]{2,1,0:T(1,128)} %reshape.350), calls=%async_computation.2 | async-start | bytes 98304 | tf_op jit(solution)/shard_map/all_to_all | solution.py:113
  306.9 79.5 %reduce-scatter.7.cloned.1.call-start = ((), (), s32[]{:S(2)}) async-start(), calls=%async_computation.7 | async-start | bytes 278528
  316.1 6.6 %copy-start.13 = (pred[16]{0:T(512)(128)(4,1)S(1)}, pred[16]{0:T(512)(128)(4,1)}, u32[]{:S(2)}) copy-start(pred[16]{0:T(512)(128)(4,1)} %copy-done.12) | copy-start | bytes 52
  316.1 6.7 %copy-start.17 = (pred[64]{0:T(512)(128)(4,1)S(1)}, pred[64]{0:T(512)(128)(4,1)}, u32[]{:S(2)}) copy-start(pred[64]{0:T(512)(128)(4,1)} %broadcast_in_dim.111) | copy-start | bytes 196
  327.3 21.6 %copy-start.20 = (u32[32]{0:T(128)S(1)}, u32[32]{0:T(128)}, u32[]{:S(2)}) copy-start(u32[32]{0:T(128)} %constant.136) | copy-start | bytes 388
  329.7 146.3 %all-reduce.6.cloned.1.call-start = ((), (), s32[]{:S(2)}) async-start(), calls=%async_computation.8 | async-start | bytes 262144
  330.8 208.5 %reduce-scatter.5.cloned.1.call-start = ((), (), s32[]{:S(2)}) async-start(), calls=%async_computation.6 | async-start | bytes 1114112 | tf_op jit(solution)/shard_map/reduce_scatter | solution.py:130
  332.9 12.5 %all-to-all-start.3 = ((bf16[16,2,192]{2,1,0:T(2,128)(2,1)}), bf16[16,2,192]{2,1,0:T(2,128)(2,1)S(1)}, u32[]{:S(2)}, u32[]{:S(2)}) async-start(bf16[16,2,192]{2,1,0:T(2,128)(2,1)} %reshape.352), calls=%async_computation.3 | async-start | bytes 32768 | tf_op jit(solution)/shard_map/all_to_all | solution.py:8
  345.4 10.0 %all-to-all-start.1 = ((bf16[2,16,384]{2,0,1:T(2,128)(2,1)}), bf16[2,16,384]{2,0,1:T(2,128)(2,1)S(1)}, u32[]{:S(2)}, u32[]{:S(2)}) async-start(bf16[2,16,384]{2,0,1:T(2,128)(2,1)} %bitcast_convert_fusion), calls=%async_computation.1 | async-start | bytes 49152 | tf_op jit(solution)/shard_map/all_to_all | solution.py:106
  (4 other events, 12.9 us)
Sparse Core Ops, SparseCore 0:
  329.8 56.5 reduce-scatter.6
  389.9 86.0 all-reduce.5
  480.2 59.0 reduce-scatter.4
